TPU v7x, 128 devices: a whole 4x4x4 slice. The times are simulated.
128 devices in a mesh: wide: 32 (over y, z, core), narrow: 4 (over x).
Axes of the slice: x: 4, y: 4, z: 4, core: 2. Of those that a mesh axis runs over, the one named last changes fastest.
Arguments:
- layer_input_rows: bfloat16 [65536, 4096], P('wide', 'narrow'), may hold values from -6 to 6
- output_gradient_rows: bfloat16 [65536, 4096], P('wide', 'narrow'), may hold values from -60 to 60
- adapter_up_weight: bfloat16 [4096, 128], P('narrow'), may hold values from -0.09375 to 0.09375
- input_side_projection: bfloat16 [4096, 128], P('narrow'), may hold values from -0.09375 to 0.09375
- rank_side_projection: bfloat16 [128, 64], replicated, may hold values from -6 to 6
- lengths: int32 [2048], P('wide'), may hold values from 1 to 32, 40960 in all
- program_output_index: int32 [2048], replicated, may hold values from 0 to 2047, each once
- targets: bfloat16 [65536, 8192], P('wide', 'narrow'), may hold values from -650 to 650
Outputs:
- scores: float32 [2048, 65536], P('narrow', 'wide')
Inputs may be any that keep to these rules, and one draw needn't show every extreme that they name: Program s uses its first lengths[s] token rows; some program uses all 32. `program_output_index`: each output row is named by exactly one program.
All inputs are finite; a program needn't handle non-finite values. No bound on the sum of `lengths` on one device may be relied on, other than what follows from the above.
Results may differ from a plain program's by a relative error of at most 0.025.
Values may be sent and summed in bfloat16 or wider, within the bound.
A program may use at most 128 MiB of HBM per device.

v0:
```python
import math
import jax
import jax.numpy as jnp
from jax import lax
from jax.sharding import PartitionSpec as P

epsilon = 1e-06
SCORE_CHUNKS = 4


def program_features(out_side, in_side, lengths, length):
    programs = lengths.shape[0]
    positions = lax.broadcasted_iota(jnp.int32, (programs, length), 1)
    live_rows = (positions < lengths[:, None]).astype(jnp.float32)
    weighted = out_side.reshape(programs, length, -1) * live_rows[:, :, None]
    inputs = in_side.reshape(programs, length, -1)
    outer_sum = jnp.einsum("sla,slb->sab", weighted, inputs, precision=lax.Precision.HIGHEST)
    return outer_sum.reshape(programs, -1)


def normalize_rows(features, squares):
    return (features * lax.rsqrt(squares + epsilon)[:, None]).astype(jnp.bfloat16)


def narrow_sum(own, send_for, count, index, link_type=jnp.bfloat16):
    total = own
    for shift in range(1, count):
        perm = [(i, (i + shift) % count) for i in range(count)]
        piece = send_for((index + shift) % count).astype(link_type)
        total = total + lax.ppermute(piece, "narrow", perm).astype(jnp.float32)
    return total


def shards(
    layer_input_rows,
    output_gradient_rows,
    adapter_up_weight,
    input_side_projection,
    rank_side_projection,
    lengths,
    program_output_index,
    targets,
):
    narrow_count = lax.axis_size("narrow")
    narrow_index = lax.axis_index("narrow")
    programs = lengths.shape[0]
    length = layer_input_rows.shape[0] // programs
    target_wide = targets.astype(jnp.float32)
    target_squares = lax.psum(jnp.sum(target_wide * target_wide, axis=1), "narrow")
    reduced_sums = jnp.dot(
        output_gradient_rows, adapter_up_weight, preferred_element_type=jnp.float32
    )
    out_part = jnp.dot(
        reduced_sums, rank_side_projection.astype(jnp.float32), precision=lax.Precision.HIGHEST
    )
    in_part = jnp.dot(layer_input_rows, input_side_projection, preferred_element_type=jnp.float32)
    quarter_cols = out_part.shape[1] // narrow_count

    def send_for(dest):
        quarter = lax.dynamic_slice_in_dim(out_part, dest * quarter_cols, quarter_cols, 1)
        return jnp.concatenate([quarter, in_part], axis=1)

    summed_parts = narrow_sum(send_for(narrow_index), send_for, narrow_count, narrow_index)
    quarter = summed_parts[:, :quarter_cols]
    in_all = summed_parts[:, quarter_cols:]
    features = program_features(quarter, in_all, lengths, length)
    squares = jnp.sum(features * features, axis=1)
    squares = narrow_sum(squares, lambda dest: squares, narrow_count, narrow_index, jnp.float32)
    unit_rows = normalize_rows(features, squares)
    target_unit = normalize_rows(target_wide, target_squares)
    row_order = jnp.argsort(program_output_index)
    contract = (((1,), (1,)), ((), ()))
    root_count = math.sqrt(float(targets.shape[1] * narrow_count))
    gathered = lax.all_gather(unit_rows, "wide", axis=0, tiled=True)
    permuted = jnp.take(gathered, row_order, axis=0)
    chunk = target_unit.shape[0] // SCORE_CHUNKS
    pieces = []
    for c in range(SCORE_CHUNKS):
        part = lax.dot_general(
            permuted,
            target_unit[c * chunk : (c + 1) * chunk],
            contract,
            preferred_element_type=jnp.float32,
        ).astype(jnp.bfloat16)
        pieces.append(
            lax.psum_scatter(part, "narrow", scatter_dimension=0, tiled=True).astype(jnp.float32)
        )
    return jnp.concatenate(pieces, axis=1) * root_count


def solution(mesh):
    return jax.shard_map(
        shards,
        mesh=mesh,
        in_specs=(
            P("wide", "narrow"),
            P("wide", "narrow"),
            P("narrow", None),
            P("narrow", None),
            P(),
            P("wide"),
            P(),
            P("wide", "narrow"),
        ),
        out_specs=P("narrow", "wide"),
        check_vma=False,
    )
```

profile of v0, /device:TPU:1, one launch (start us, length us, event | category | flops | bytes accessed | tf_op | source)
XLA Modules:
  0.0 278.4 jit_solution(10977193983828737708)
XLA Ops:
  6.5 3.6 %fusion.14 = f32[2048,128]{1,0:T(8,128)S(1)} fusion(bf16[2048,1024]{1,0:T(8,128)(2,1)} %param.9, bf16[1024,128]{1,0:T(8,128)(2,1)} %param.10), kind=kOutput, calls=%fused_computation.39 | convolution fusion | flops 536870912 | bytes 5505024 | tf_op jit(solution)/shard_map/dot_general | solution.py:50
  11.0 1.5 fusion.13
  13.6 2.0 collective-permute-start
  15.6 2.5 collective-permute-start.1
  19.3 10.5 %collective-permute-done = bf16[2048,144]{0,1:T(8,128)(2,1)} collective-permute-done((bf16[2048,144]{0,1:T(8,128)(2,1)}, bf16[2048,144]{0,1:T(8,128)(2,1)}, u32[]{:S(2)}, u32[]{:S(2)}) %collective-permute-start) | collective-permute-done | bytes 589856 | tf_op jit(solution)/shard_map/ppermute | solution.py:30
  29.8 13.9 %collective-permute-done.1 = bf16[2048,144]{0,1:T(8,128)(2,1)} collective-permute-done((bf16[2048,144]{0,1:T(8,128)(2,1)S(1)}, bf16[2048,144]{0,1:T(8,128)(2,1)}, u32[]{:S(2)}, u32[]{:S(2)}) %collective-permute-start.1) | collective-permute-done | bytes 589856 | tf_op jit(solution)/shard_map/ppermute | solution.py:30
  43.8 1.7 fusion.7
  46.2 1.7 multiply_reduce_fusion
  48.7 3.0 %collective-permute-start.4 = (f32[64]{0:T(128)S(1)}, f32[64]{0:T(128)S(1)}, u32[]{:S(2)}, u32[]{:S(2)}) collective-permute-start(f32[64]{0:T(128)S(1)} %get-tuple-element.15), channel_id=1, source_target_pairs={{0,2},{1,3},{2,0},{3,1},{4,6},{5,7},{6,4},{7,5},{8,10},{9,11},{10,... | collective-permute-start | bytes 776 | tf_op jit(solution)/shard_map/ppermute | solution.py:30
  52.7 1.5 collective-permute-done.5
  55.2 5.0 %sort.17 = (s32[2048]{0:T(1024)}, s32[2048]{0:T(1024)S(1)}) sort(s32[2048]{0:T(1024)S(1)} %copy-done.4, s32[2048]{0:T(1024)S(1)} %iota.11), dimensions={0}, to_apply=%region_0.0 | sort | flops 22528 | bytes 32768 | tf_op jit(solution)/shard_map/jit(argsort)/sort | solution.py:71
  60.2 5.1 %fusion = f32[2048]{0:T(1024)S(1)} fusion(bf16[2048,2048]{1,0:T(8,128)(2,1)} %param.15), kind=kLoop, calls=%fused_computation.3 | loop fusion | flops 12580864 | bytes 8396800 | tf_op jit(solution)/shard_map/reduce_sum | solution.py:49
  65.3 7.6 %psum.7 = f32[2048]{0:T(1024)S(1)} all-reduce(f32[2048]{0:T(1024)S(1)} %fusion), channel_id=1, replica_groups=mesh['wide'=32,'narrow'=4] {'narrow'}, use_global_device_ids=true, to_apply=%region_3.4 | all-reduce | flops 2048 | bytes 16384 | tf_op jit(solution)/shard_map/psum | solution.py:49
  73.0 8.1 %fusion.1 = bf16[2048,2048]{1,0:T(8,128)(2,1)} fusion(bf16[2048,2048]{1,0:T(8,128)(2,1)} %param.15, f32[2048]{0:T(1024)S(1)} %add_rsqrt_fusion), kind=kLoop, calls=%fused_computation.4 | loop fusion | flops 12582912 | bytes 16785408 | tf_op jit(solution)/shard_map/convert_element_type | solution.py:22
  81.1 31.5 %all-gather.2.cloned.1.call-done = bf16[2048,2048]{1,0:T(8,128)(2,1)} async-done(((bf16[64,2048]{1,0:T(8,128)(2,1)}), bf16[2048,2048]{1,0:T(8,128)(2,1)}) %all-gather.2.cloned.1.call-update) | async-done | bytes 8388624 | tf_op jit(solution)/shard_map/all_gather | solution.py:74
  112.5 20.8 %gather_fusion = bf16[2048,2048]{1,0:T(8,128)(2,1)} fusion(bf16[2048,2048]{1,0:T(8,128)(2,1)} %all-gather.2.cloned.1.call-done, s32[2048]{0:T(1024)S(1)} %fusion.12), kind=kCustom, calls=%fused_computation | custom fusion | bytes 16785408 | tf_op jit(solution)/shard_map/jit(_take)/gather | solution.py:75
  133.3 10.1 %convolution_convert_fusion.3 = bf16[2048,512]{1,0:T(8,128)(2,1)} fusion(bf16[2048,2048]{1,0:T(8,128)(2,1)} %fusion.1, bf16[2048,2048]{1,0:T(8,128)(2,1)} %gather_fusion, pred[2048]{0:T(1024)(128)(4,1)S(1)} %compare_and_fusion), kind=kOutput, calls=%fused_computation.10 | convolution fusion | flops 4300210176 | bytes 12584960 | tf_op jit(solution)/shard_map/dot_general | solution.py:79
  143.7 10.1 %convolution_convert_fusion.2 = bf16[2048,512]{1,0:T(8,128)(2,1)} fusion(bf16[2048,2048]{1,0:T(8,128)(2,1)} %fusion.1, bf16[2048,2048]{1,0:T(8,128)(2,1)} %gather_fusion, pred[2048]{0:T(1024)(128)(4,1)S(1)} %compare_and_fusion), kind=kOutput, calls=%fused_computation.9 | convolution fusion | flops 4300210176 | bytes 12584960 | tf_op jit(solution)/shard_map/dot_general | solution.py:79
  153.9 10.1 %convolution_convert_fusion.1 = bf16[2048,512]{1,0:T(8,128)(2,1)} fusion(bf16[2048,2048]{1,0:T(8,128)(2,1)} %fusion.1, bf16[2048,2048]{1,0:T(8,128)(2,1)} %gather_fusion, pred[2048]{0:T(1024)(128)(4,1)S(1)} %compare_and_fusion), kind=kOutput, calls=%fused_computation.8 | convolution fusion | flops 4300210176 | bytes 12584960 | tf_op jit(solution)/shard_map/dot_general | solution.py:79
  164.4 10.1 %convolution_convert_fusion = bf16[2048,512]{1,0:T(8,128)(2,1)} fusion(bf16[2048,2048]{1,0:T(8,128)(2,1)} %fusion.1, bf16[2048,2048]{1,0:T(8,128)(2,1)} %gather_fusion, pred[2048]{0:T(1024)(128)(4,1)S(1)} %compare_and_fusion), kind=kOutput, calls=%fused_computation.7 | convolution fusion | flops 4300210176 | bytes 12584960 | tf_op jit(solution)/shard_map/dot_general | solution.py:79
  174.6 29.8 %reduce-scatter.7.cloned.1.call-done = bf16[512,512]{1,0:T(8,128)(2,1)} async-done(((bf16[2048,512]{1,0:T(8,128)(2,1)}), bf16[512,512]{1,0:T(8,128)(2,1)}) %reduce-scatter.7.cloned.1.call-update) | async-done | bytes 524304 | tf_op jit(solution)/shard_map/reduce_scatter | solution.py:86
  204.3 31.7 %reduce-scatter.9.cloned.1.call-done = bf16[512,512]{1,0:T(8,128)(2,1)} async-done(((bf16[2048,512]{1,0:T(8,128)(2,1)}), bf16[512,512]{1,0:T(8,128)(2,1)}) %reduce-scatter.9.cloned.1.call-update) | async-done | bytes 524304 | tf_op jit(solution)/shard_map/reduce_scatter | solution.py:86
  236.0 31.8 %reduce-scatter.11.cloned.1.call-done = bf16[512,512]{1,0:T(8,128)(2,1)} async-done(((bf16[2048,512]{1,0:T(8,128)(2,1)}), bf16[512,512]{1,0:T(8,128)(2,1)}) %reduce-scatter.11.cloned.1.call-update) | async-done | bytes 524304 | tf_op jit(solution)/shard_map/reduce_scatter | solution.py:86
  267.8 4.1 %convert_multiply_fusion.2 = f32[512,2048]{1,0:T(8,128)} fusion(bf16[512,512]{1,0:T(8,128)(2,1)} %reduce-scatter.11.cloned.1.call-done, bf16[512,512]{1,0:T(8,128)(2,1)} %reduce-scatter.9.cloned.1.call-done, bf16[512,512]{1,0:T(8,128)(2,1)} %reduce-scatter.7.cloned.1.call-done, bf16[512,512]{1,0:T(8,128)(2,1)} %reduce-scatter.5.cloned.1.call-done), kind=kLoop, calls=%fused_computation.6 | loop fusion | flops 9437184 | bytes 6291456 | tf_op jit(solution)/shard_map/mul | solution.py:88
  (45 shorter events, 7.1 us)
Async XLA Ops:
  6.5 4.4 %copy-start = (bf16[1024,128]{1,0:T(8,128)(2,1)S(1)}, bf16[1024,128]{1,0:T(8,128)(2,1)}, u32[]{:S(2)}) copy-start(bf16[1024,128]{1,0:T(8,128)(2,1)} %param.11) | copy-start | bytes 786436
  6.5 3.6 %copy-start.3 = (bf16[128,64]{0,1:T(8,128)(2,1)S(1)}, bf16[128,64]{0,1:T(8,128)(2,1)}, u32[]{:S(2)}) copy-start(bf16[128,64]{0,1:T(8,128)(2,1)} %param.12) | copy-start | bytes 49156
  6.5 106.0 %all-gather.2.cloned.1.call-start = ((), (), s32[]{:S(2)}) async-start(), calls=%async_computation.4 | async-start | bytes 8650752 | tf_op jit(solution)/shard_map/all_gather | solution.py:74
  6.5 4.4 %copy-start.2 = (bf16[2048,1024]{1,0:T(8,128)(2,1)S(1)}, bf16[2048,1024]{1,0:T(8,128)(2,1)}, u32[]{:S(2)}) copy-start(bf16[2048,1024]{1,0:T(8,128)(2,1)} %param.8) | copy-start | bytes 12582916
  11.0 8.3 %copy-start.5 = (s32[64]{0:T(128)S(1)}, s32[64]{0:T(128)}, u32[]{:S(2)}) copy-start(s32[64]{0:T(128)} %param.13) | copy-start | bytes 772
  13.6 16.2 %collective-permute-start = (bf16[2048,144]{0,1:T(8,128)(2,1)}, bf16[2048,144]{0,1:T(8,128)(2,1)}, u32[]{:S(2)}, u32[]{:S(2)}) collective-permute-start(bf16[2048,144]{0,1:T(8,128)(2,1)} %get-tuple-element.7), channel_id=1, source_target_pairs={{0,1},{1,2},{2,3},{3,0},{4,5},{5,6},{6,7},{7,4},{8,9},{9,10},{10,1... | collective-permute-start | bytes 1769480 | tf_op jit(solution)/shard_map/ppermute | solution.py:30
  15.6 28.1 %collective-permute-start.1 = (bf16[2048,144]{0,1:T(8,128)(2,1)S(1)}, bf16[2048,144]{0,1:T(8,128)(2,1)}, u32[]{:S(2)}, u32[]{:S(2)}) collective-permute-start(bf16[2048,144]{0,1:T(8,128)(2,1)S(1)} %get-tuple-element.8), channel_id=1, source_target_pairs={{0,2},{1,3},{2,0},{3,1},{4,6},{5,7},{6,4},{7,5},{8,10},{9,11},{10,... | collective-permute-start | bytes 1769480 | tf_op jit(solution)/shard_map/ppermute | solution.py:30
  18.1 25.7 %collective-permute-start.2 = (bf16[2048,144]{0,1:T(8,128)(2,1)S(1)}, bf16[2048,144]{0,1:T(8,128)(2,1)}, u32[]{:S(2)}, u32[]{:S(2)}) collective-permute-start(bf16[2048,144]{0,1:T(8,128)(2,1)S(1)} %get-tuple-element.9), channel_id=1, source_target_pairs={{0,3},{1,0},{2,1},{3,2},{4,7},{5,4},{6,5},{7,6},{8,11},{9,8},{10,9... | collective-permute-start | bytes 1769480 | tf_op jit(solution)/shard_map/ppermute | solution.py:30
  45.5 9.6 %copy-start.4 = (s32[2048]{0:T(1024)S(1)}, s32[2048]{0:T(1024)}, u32[]{:S(2)}) copy-start(s32[2048]{0:T(1024)} %param.14) | copy-start | bytes 24580
  47.9 4.0 %collective-permute-start.3 = (f32[64]{0:T(128)S(1)}, f32[64]{0:T(128)S(1)}, u32[]{:S(2)}, u32[]{:S(2)}) collective-permute-start(f32[64]{0:T(128)S(1)} %get-tuple-element.15), channel_id=1, source_target_pairs={{0,1},{1,2},{2,3},{3,0},{4,5},{5,6},{6,7},{7,4},{8,9},{9,10},{10,1... | collective-permute-start | bytes 776 | tf_op jit(solution)/shard_map/ppermute | solution.py:30
  48.7 4.0 %collective-permute-start.4 = (f32[64]{0:T(128)S(1)}, f32[64]{0:T(128)S(1)}, u32[]{:S(2)}, u32[]{:S(2)}) collective-permute-start(f32[64]{0:T(128)S(1)} %get-tuple-element.15), channel_id=1, source_target_pairs={{0,2},{1,3},{2,0},{3,1},{4,6},{5,7},{6,4},{7,5},{8,10},{9,11},{10,... | collective-permute-start | bytes 776 | tf_op jit(solution)/shard_map/ppermute | solution.py:30
  51.8 2.4 collective-permute-start.5
  55.1 119.5 %reduce-scatter.5.cloned.1.call-start = ((), (), s32[]{:S(2)}) async-start(), calls=%async_computation.5 | async-start | bytes 2621440 | tf_op jit(solution)/shard_map/reduce_scatter | solution.py:86
  143.5 60.9 %reduce-scatter.7.cloned.1.call-start = ((), (), s32[]{:S(2)}) async-start(), calls=%async_computation.6 | async-start | bytes 2621440 | tf_op jit(solution)/shard_map/reduce_scatter | solution.py:86
  153.9 82.2 %reduce-scatter.9.cloned.1.call-start = ((), (), s32[]{:S(2)}) async-start(), calls=%async_computation.7 | async-start | bytes 2621440 | tf_op jit(solution)/shard_map/reduce_scatter | solution.py:86
  164.1 103.8 %reduce-scatter.11.cloned.1.call-start = ((), (), s32[]{:S(2)}) async-start(), calls=%async_computation.8 | async-start | bytes 2621440 | tf_op jit(solution)/shard_map/reduce_scatter | solution.py:86
  174.5 97.4 %copy-start.1 = (bf16[1024,128]{1,0:T(8,128)(2,1)S(1)}, bf16[1024,128]{1,0:T(8,128)(2,1)}, u32[]{:S(2)}) copy-start(bf16[1024,128]{1,0:T(8,128)(2,1)} %param.11) | copy-start | bytes 786436
Sparse Core Ops, SparseCore 0:
  55.2 57.2 all-gather.1
  143.6 28.7 reduce-scatter.4
  174.9 29.3 reduce-scatter.6
  206.6 29.3 reduce-scatter.8
  238.4 29.3 reduce-scatter.10
where the time goes:
time: 279 us; the launch traced here: 278 us
  waiting for transfers between devices  152 us (54%)
  matrix products  48.1 us (17%)
  other arithmetic  26.1 us (9%)
  local copies, waits for them, and re-layouts  21.5 us (8%)
  between operations  13.3 us (5%)
  starting transfers between devices  10.3 us (4%)
  blocking collectives  7.64 us (3%)
    reduce_scatter x4, waiting for transfers between devices, shards(): lax.psum_scatter(part, 'narrow', scatter_dimension=0, tiled=True)  93.3 us
    dot_general x4, matrix products, shards(): lax.dot_general(permuted, target_unit[c * chunk:(c + 1) * chunk], contrac...  40.5 us
    all_gather x1, waiting for transfers between devices, shards(): gathered = lax.all_gather(unit_rows, 'wide', axis=0, tiled=True)  31.5 us
    ppermute x6, waiting for transfers between devices, narrow_sum(): total = total + lax.ppermute(piece, 'narrow', perm).astype(jnp.float32)  26.7 us
    gather x1, local copies, waits for them, and re-layouts, shards(): permuted = jnp.take(gathered, row_order, axis=0)  20.8 us
    ppermute x6, starting transfers between devices, narrow_sum(): total = total + lax.ppermute(piece, 'narrow', perm).astype(jnp.float32)  9.65 us
    convert_element_type x2, other arithmetic, normalize_rows(): (features * lax.rsqrt(squares + epsilon)[:, None]).astype(jnp.bfloat16)  9 us
    psum x1, blocking collectives, shards(): lax.psum(jnp.sum(target_wide * target_wide, axis=1), 'narrow')  7.64 us
  transfers between devices with their start and end apart: 11, of which 8 were waited for; matrix products, arithmetic and copies ran while one was open for 17% of the time, Pallas kernels for 0%

commit v1 on v0

--- a/solution.py
+++ b/solution.py
@@ -71,7 +71,9 @@
     row_order = jnp.argsort(program_output_index)
     contract = (((1,), (1,)), ((), ()))
     root_count = math.sqrt(float(targets.shape[1] * narrow_count))
-    gathered = lax.all_gather(unit_rows, "wide", axis=0, tiled=True)
+    gathered = jnp.concatenate(
+        lax.all_to_all(jnp.stack([unit_rows] * lax.axis_size("wide")), "wide", 0, 0), axis=0
+    )
     permuted = jnp.take(gathered, row_order, axis=0)
     chunk = target_unit.shape[0] // SCORE_CHUNKS
     pieces = []

time: 279 us -> 360 us (1.29)
  waiting for transfers between devices: 152 us -> 216 us
  starting transfers between devices: 10.3 us -> 21 us
  local copies, waits for them, and re-layouts: 21.5 us -> 25.7 us
    all_to_all x0 -> x1, waiting for transfers between devices: none -> 80.7 us  [shards(): lax.all_to_all(jnp.stack([unit_rows] * lax.axis_size('wide')), 'wide', 0, 0)]
    all_gather x1 -> x0, waiting for transfers between devices: 31.5 us -> none  [shards(): gathered = lax.all_gather(unit_rows, 'wide', axis=0, tiled=True)]
    reduce_scatter x4, waiting for transfers between devices: 93.3 us -> 109 us  [shards(): lax.psum_scatter(part, 'narrow', scatter_dimension=0, tiled=True)]
    all_to_all x0 -> x1, starting transfers between devices: none -> 10.7 us  [shards(): lax.all_to_all(jnp.stack([unit_rows] * lax.axis_size('wide')), 'wide', 0, 0)]
    another operation x1 -> x2, local copies, waits for them, and re-layouts: 0.03 us -> 4.31 us  [the longest x1 4.28 us: shards(): jnp.stack([unit_rows] * lax.axis_size('wide'))]
  transfers between devices with their start and end apart: 11 -> 11, of which waited for: 8 -> 9; matrix products, arithmetic and copies ran while one was open for 17% -> 14% of each run, Pallas kernels for 0% -> 0%
where the time goes in v1:
time: 360 us
  waiting for transfers between devices  216 us (60%)
  matrix products  48.3 us (13%)
  local copies, waits for them, and re-layouts  25.7 us (7%)
  other arithmetic  25.3 us (7%)
  starting transfers between devices  21 us (6%)
  between operations  13.3 us (4%)
  blocking collectives  9.59 us (3%)
    reduce_scatter x4, waiting for transfers between devices, shards(): lax.psum_scatter(part, 'narrow', scatter_dimension=0, tiled=True)  109 us
    all_to_all x1, waiting for transfers between devices, shards(): lax.all_to_all(jnp.stack([unit_rows] * lax.axis_size('wide')), 'wide', 0, 0)  80.7 us
    dot_general x4, matrix products, shards(): lax.dot_general(permuted, target_unit[c * chunk:(c + 1) * chunk], contrac...  40.7 us
    ppermute x6, waiting for transfers between devices, narrow_sum(): total = total + lax.ppermute(piece, 'narrow', perm).astype(jnp.float32)  26.7 us
    gather x1, local copies, waits for them, and re-layouts, shards(): permuted = jnp.take(gathered, row_order, axis=0)  20.8 us
    all_to_all x1, starting transfers between devices, shards(): lax.all_to_all(jnp.stack([unit_rows] * lax.axis_size('wide')), 'wide', 0, 0)  10.7 us
    ppermute x6, starting transfers between devices, narrow_sum(): total = total + lax.ppermute(piece, 'narrow', perm).astype(jnp.float32)  9.66 us
    psum x1, blocking collectives, shards(): lax.psum(jnp.sum(target_wide * target_wide, axis=1), 'narrow')  9.59 us
  transfers between devices with their start and end apart: 11, of which 9 were waited for; matrix products, arithmetic and copies ran while one was open for 14% of the time, Pallas kernels for 0%

profile of v1, /device:TPU:1, one launch (start us, length us, event | category | flops | bytes accessed | tf_op | source)
XLA Modules:
  0.0 359.6 jit_solution(1097506254515160845)
XLA Ops:
  6.5 3.6 %fusion.14 = f32[2048,128]{1,0:T(8,128)S(1)} fusion(bf16[2048,1024]{1,0:T(8,128)(2,1)} %param.9, bf16[1024,128]{1,0:T(8,128)(2,1)} %param.10), kind=kOutput, calls=%fused_computation.39 | convolution fusion | flops 536870912 | bytes 5505024 | tf_op jit(solution)/shard_map/dot_general | solution.py:50
  13.6 2.0 collective-permute-start
  15.6 2.5 collective-permute-start.1
  19.3 10.5 %collective-permute-done = bf16[2048,144]{0,1:T(8,128)(2,1)} collective-permute-done((bf16[2048,144]{0,1:T(8,128)(2,1)}, bf16[2048,144]{0,1:T(8,128)(2,1)}, u32[]{:S(2)}, u32[]{:S(2)}) %collective-permute-start) | collective-permute-done | bytes 589856 | tf_op jit(solution)/shard_map/ppermute | solution.py:30
  29.8 14.0 %collective-permute-done.1 = bf16[2048,144]{0,1:T(8,128)(2,1)} collective-permute-done((bf16[2048,144]{0,1:T(8,128)(2,1)S(1)}, bf16[2048,144]{0,1:T(8,128)(2,1)}, u32[]{:S(2)}, u32[]{:S(2)}) %collective-permute-start.1) | collective-permute-done | bytes 589856 | tf_op jit(solution)/shard_map/ppermute | solution.py:30
  46.2 1.7 multiply_reduce_fusion
  48.7 3.0 collective-permute-start.4
  54.3 4.3 %stack.2 = bf16[32,64,2048]{2,1,0:T(8,128)(2,1)} broadcast(bf16[64,2048]{1,0:T(8,128)(2,1)S(1)} %fusion.8), dimensions={1,2} | broadcast | bytes 8650752 | tf_op jit(solution)/shard_map/stack | solution.py:75
  58.6 10.7 %all-to-all-start = ((bf16[32,64,2048]{2,1,0:T(8,128)(2,1)}), bf16[32,64,2048]{2,1,0:T(8,128)(2,1)}, u32[]{:S(2)}, u32[]{:S(2)}) async-start(bf16[32,64,2048]{2,1,0:T(8,128)(2,1)} %stack.2), calls=%async_computation | async-start | bytes 16777216 | tf_op jit(solution)/shard_map/all_to_all | solution.py:75
  69.4 5.0 %sort.17 = (s32[2048]{0:T(1024)}, s32[2048]{0:T(1024)S(1)}) sort(s32[2048]{0:T(1024)S(1)} %copy-done.4, s32[2048]{0:T(1024)S(1)} %iota.11), dimensions={0}, to_apply=%region_0.0 | sort | flops 22528 | bytes 32768 | tf_op jit(solution)/shard_map/jit(argsort)/sort | solution.py:71
  74.4 5.1 %fusion = f32[2048]{0:T(1024)S(1)} fusion(bf16[2048,2048]{1,0:T(8,128)(2,1)} %param.15), kind=kLoop, calls=%fused_computation.3 | loop fusion | flops 12580864 | bytes 8396800 | tf_op jit(solution)/shard_map/reduce_sum | solution.py:49
  79.5 9.6 %psum.7 = f32[2048]{0:T(1024)S(1)} all-reduce(f32[2048]{0:T(1024)S(1)} %fusion), channel_id=1, replica_groups=mesh['wide'=32,'narrow'=4] {'narrow'}, use_global_device_ids=true, to_apply=%region_3.4 | all-reduce | flops 2048 | bytes 16384 | tf_op jit(solution)/shard_map/psum | solution.py:49
  89.1 8.0 %fusion.1 = bf16[2048,2048]{1,0:T(8,128)(2,1)} fusion(bf16[2048,2048]{1,0:T(8,128)(2,1)} %param.15, f32[2048]{0:T(1024)S(1)} %add_rsqrt_fusion), kind=kLoop, calls=%fused_computation.4 | loop fusion | flops 12582912 | bytes 16785408 | tf_op jit(solution)/shard_map/convert_element_type | solution.py:22
  97.1 80.7 %all-to-all-done = bf16[32,64,2048]{2,1,0:T(8,128)(2,1)} async-done(((bf16[32,64,2048]{2,1,0:T(8,128)(2,1)}), bf16[32,64,2048]{2,1,0:T(8,128)(2,1)}, u32[]{:S(2)}, u32[]{:S(2)}) %all-to-all-start) | async-done | bytes 8388640 | tf_op jit(solution)/shard_map/all_to_all | solution.py:75
  177.8 20.8 %gather_fusion = bf16[2048,2048]{1,0:T(8,128)(2,1)} fusion(bf16[2048,2048]{1,0:T(8,128)(2,1)} %bitcast.1, s32[2048]{0:T(1024)S(1)} %fusion.12), kind=kCustom, calls=%fused_computation | custom fusion | bytes 16785408 | tf_op jit(solution)/shard_map/jit(_take)/gather | solution.py:77
  198.6 10.1 %convolution_convert_fusion.3 = bf16[2048,512]{1,0:T(8,128)(2,1)} fusion(bf16[2048,2048]{1,0:T(8,128)(2,1)} %fusion.1, bf16[2048,2048]{1,0:T(8,128)(2,1)} %gather_fusion, pred[2048]{0:T(1024)(128)(4,1)S(1)} %compare_and_fusion), kind=kOutput, calls=%fused_computation.10 | convolution fusion | flops 4300210176 | bytes 12584960 | tf_op jit(solution)/shard_map/dot_general | solution.py:81
  209.0 10.1 %convolution_convert_fusion.2 = bf16[2048,512]{1,0:T(8,128)(2,1)} fusion(bf16[2048,2048]{1,0:T(8,128)(2,1)} %fusion.1, bf16[2048,2048]{1,0:T(8,128)(2,1)} %gather_fusion, pred[2048]{0:T(1024)(128)(4,1)S(1)} %compare_and_fusion), kind=kOutput, calls=%fused_computation.9 | convolution fusion | flops 4300210176 | bytes 12584960 | tf_op jit(solution)/shard_map/dot_general | solution.py:81
  219.2 10.1 %convolution_convert_fusion.1 = bf16[2048,512]{1,0:T(8,128)(2,1)} fusion(bf16[2048,2048]{1,0:T(8,128)(2,1)} %fusion.1, bf16[2048,2048]{1,0:T(8,128)(2,1)} %gather_fusion, pred[2048]{0:T(1024)(128)(4,1)S(1)} %compare_and_fusion), kind=kOutput, calls=%fused_computation.8 | convolution fusion | flops 4300210176 | bytes 12584960 | tf_op jit(solution)/shard_map/dot_general | solution.py:81
  229.6 10.5 %convolution_convert_fusion = bf16[2048,512]{1,0:T(8,128)(2,1)} fusion(bf16[2048,2048]{1,0:T(8,128)(2,1)} %fusion.1, bf16[2048,2048]{1,0:T(8,128)(2,1)} %gather_fusion, pred[2048]{0:T(1024)(128)(4,1)S(1)} %compare_and_fusion), kind=kOutput, calls=%fused_computation.7 | convolution fusion | flops 4300210176 | bytes 12584960 | tf_op jit(solution)/shard_map/dot_general | solution.py:81
  240.1 13.3 %reduce-scatter.5.cloned.1.call-done = bf16[512,512]{1,0:T(8,128)(2,1)} async-done(((bf16[2048,512]{1,0:T(8,128)(2,1)}), bf16[512,512]{1,0:T(8,128)(2,1)}) %reduce-scatter.5.cloned.1.call-update) | async-done | bytes 524304 | tf_op jit(solution)/shard_map/reduce_scatter | solution.py:88
  253.4 32.0 %reduce-scatter.7.cloned.1.call-done = bf16[512,512]{1,0:T(8,128)(2,1)} async-done(((bf16[2048,512]{1,0:T(8,128)(2,1)}), bf16[512,512]{1,0:T(8,128)(2,1)}) %reduce-scatter.7.cloned.1.call-update) | async-done | bytes 524304 | tf_op jit(solution)/shard_map/reduce_scatter | solution.py:88
  285.4 31.8 %reduce-scatter.9.cloned.1.call-done = bf16[512,512]{1,0:T(8,128)(2,1)} async-done(((bf16[2048,512]{1,0:T(8,128)(2,1)}), bf16[512,512]{1,0:T(8,128)(2,1)}) %reduce-scatter.9.cloned.1.call-update) | async-done | bytes 524304 | tf_op jit(solution)/shard_map/reduce_scatter | solution.py:88
  317.2 31.8 %reduce-scatter.11.cloned.1.call-done = bf16[512,512]{1,0:T(8,128)(2,1)} async-done(((bf16[2048,512]{1,0:T(8,128)(2,1)}), bf16[512,512]{1,0:T(8,128)(2,1)}) %reduce-scatter.11.cloned.1.call-update) | async-done | bytes 524304 | tf_op jit(solution)/shard_map/reduce_scatter | solution.py:88
  349.0 4.1 %convert_multiply_fusion.2 = f32[512,2048]{1,0:T(8,128)} fusion(bf16[512,512]{1,0:T(8,128)(2,1)} %reduce-scatter.11.cloned.1.call-done, bf16[512,512]{1,0:T(8,128)(2,1)} %reduce-scatter.9.cloned.1.call-done, bf16[512,512]{1,0:T(8,128)(2,1)} %reduce-scatter.7.cloned.1.call-done, bf16[512,512]{1,0:T(8,128)(2,1)} %reduce-scatter.5.cloned.1.call-done), kind=kLoop, calls=%fused_computation.6 | loop fusion | flops 9437184 | bytes 6291456 | tf_op jit(solution)/shard_map/mul | solution.py:90
  (45 shorter events, 11.1 us)
Async XLA Ops:
  6.5 4.4 %copy-start = (bf16[1024,128]{1,0:T(8,128)(2,1)S(1)}, bf16[1024,128]{1,0:T(8,128)(2,1)}, u32[]{:S(2)}) copy-start(bf16[1024,128]{1,0:T(8,128)(2,1)} %param.11) | copy-start | bytes 786436
  6.5 3.6 %copy-start.3 = (bf16[128,64]{0,1:T(8,128)(2,1)S(1)}, bf16[128,64]{0,1:T(8,128)(2,1)}, u32[]{:S(2)}) copy-start(bf16[128,64]{0,1:T(8,128)(2,1)} %param.12) | copy-start | bytes 49156
  6.5 4.4 %copy-start.2 = (bf16[2048,1024]{1,0:T(8,128)(2,1)S(1)}, bf16[2048,1024]{1,0:T(8,128)(2,1)}, u32[]{:S(2)}) copy-start(bf16[2048,1024]{1,0:T(8,128)(2,1)} %param.8) | copy-start | bytes 12582916
  10.9 8.3 %copy-start.5 = (s32[64]{0:T(128)S(1)}, s32[64]{0:T(128)}, u32[]{:S(2)}) copy-start(s32[64]{0:T(128)} %param.13) | copy-start | bytes 772
  13.6 16.2 %collective-permute-start = (bf16[2048,144]{0,1:T(8,128)(2,1)}, bf16[2048,144]{0,1:T(8,128)(2,1)}, u32[]{:S(2)}, u32[]{:S(2)}) collective-permute-start(bf16[2048,144]{0,1:T(8,128)(2,1)} %get-tuple-element.7), channel_id=1, source_target_pairs={{0,1},{1,2},{2,3},{3,0},{4,5},{5,6},{6,7},{7,4},{8,9},{9,10},{10,1... | collective-permute-start | bytes 1769480 | tf_op jit(solution)/shard_map/ppermute | solution.py:30
  15.6 28.1 %collective-permute-start.1 = (bf16[2048,144]{0,1:T(8,128)(2,1)S(1)}, bf16[2048,144]{0,1:T(8,128)(2,1)}, u32[]{:S(2)}, u32[]{:S(2)}) collective-permute-start(bf16[2048,144]{0,1:T(8,128)(2,1)S(1)} %get-tuple-element.8), channel_id=1, source_target_pairs={{0,2},{1,3},{2,0},{3,1},{4,6},{5,7},{6,4},{7,5},{8,10},{9,11},{10,... | collective-permute-start | bytes 1769480 | tf_op jit(solution)/shard_map/ppermute | solution.py:30
  18.1 25.7 %collective-permute-start.2 = (bf16[2048,144]{0,1:T(8,128)(2,1)S(1)}, bf16[2048,144]{0,1:T(8,128)(2,1)}, u32[]{:S(2)}, u32[]{:S(2)}) collective-permute-start(bf16[2048,144]{0,1:T(8,128)(2,1)S(1)} %get-tuple-element.9), channel_id=1, source_target_pairs={{0,3},{1,0},{2,1},{3,2},{4,7},{5,4},{6,5},{7,6},{8,11},{9,8},{10,9... | collective-permute-start | bytes 1769480 | tf_op jit(solution)/shard_map/ppermute | solution.py:30
  47.9 4.0 %collective-permute-start.3 = (f32[64]{0:T(128)S(1)}, f32[64]{0:T(128)S(1)}, u32[]{:S(2)}, u32[]{:S(2)}) collective-permute-start(f32[64]{0:T(128)S(1)} %get-tuple-element.15), channel_id=1, source_target_pairs={{0,1},{1,2},{2,3},{3,0},{4,5},{5,6},{6,7},{7,4},{8,9},{9,10},{10,1... | collective-permute-start | bytes 776 | tf_op jit(solution)/shard_map/ppermute | solution.py:30
  48.7 4.0 %collective-permute-start.4 = (f32[64]{0:T(128)S(1)}, f32[64]{0:T(128)S(1)}, u32[]{:S(2)}, u32[]{:S(2)}) collective-permute-start(f32[64]{0:T(128)S(1)} %get-tuple-element.15), channel_id=1, source_target_pairs={{0,2},{1,3},{2,0},{3,1},{4,6},{5,7},{6,4},{7,5},{8,10},{9,11},{10,... | collective-permute-start | bytes 776 | tf_op jit(solution)/shard_map/ppermute | solution.py:30
  51.8 2.4 collective-permute-start.5
  58.6 10.7 %copy-start.4 = (s32[2048]{0:T(1024)S(1)}, s32[2048]{0:T(1024)}, u32[]{:S(2)}) copy-start(s32[2048]{0:T(1024)} %param.14) | copy-start | bytes 24580
  58.6 119.2 %all-to-all-start = ((bf16[32,64,2048]{2,1,0:T(8,128)(2,1)}), bf16[32,64,2048]{2,1,0:T(8,128)(2,1)}, u32[]{:S(2)}, u32[]{:S(2)}) async-start(bf16[32,64,2048]{2,1,0:T(8,128)(2,1)} %stack.2), calls=%async_computation | async-start | bytes 16777216 | tf_op jit(solution)/shard_map/all_to_all | solution.py:75
  69.3 184.1 %reduce-scatter.5.cloned.1.call-start = ((), (), s32[]{:S(2)}) async-start(), calls=%async_computation.5 | async-start | bytes 2621440 | tf_op jit(solution)/shard_map/reduce_scatter | solution.py:88
  208.8 76.6 %reduce-scatter.7.cloned.1.call-start = ((), (), s32[]{:S(2)}) async-start(), calls=%async_computation.6 | async-start | bytes 2621440 | tf_op jit(solution)/shard_map/reduce_scatter | solution.py:88
  219.1 98.1 %reduce-scatter.9.cloned.1.call-start = ((), (), s32[]{:S(2)}) async-start(), calls=%async_computation.7 | async-start | bytes 2621440 | tf_op jit(solution)/shard_map/reduce_scatter | solution.py:88
  229.3 119.7 %reduce-scatter.11.cloned.1.call-start = ((), (), s32[]{:S(2)}) async-start(), calls=%async_computation.8 | async-start | bytes 2621440 | tf_op jit(solution)/shard_map/reduce_scatter | solution.py:88
  240.1 113.1 %copy-start.1 = (bf16[1024,128]{1,0:T(8,128)(2,1)S(1)}, bf16[1024,128]{1,0:T(8,128)(2,1)}, u32[]{:S(2)}) copy-start(bf16[1024,128]{1,0:T(8,128)(2,1)} %param.11) | copy-start | bytes 786436
Sparse Core Ops, SparseCore 0:
  208.9 44.4 reduce-scatter.4
  255.9 29.3 reduce-scatter.6
  287.8 29.3 reduce-scatter.8
  319.6 29.3 reduce-scatter.10
